TPU v7x, 32 devices: a whole 2x2x4 slice. The times are simulated.
32 devices in a mesh: seq: 8 (over z, y), head: 4 (over x, core).
Axes of the slice: x: 2, y: 2, z: 4, core: 2. Of those that a mesh axis runs over, the one named last changes fastest.
Arguments:
- queries: bfloat16 [2048, 2048], P('seq', 'head'), may hold values from -6 to 6
- keys: bfloat16 [2048, 2048], P('seq', 'head'), may hold values from -40 to 40
- values: bfloat16 [2048, 2048], P('seq', 'head'), may hold values from -24 to 24
- ridges: float32 [16], P('head'), may hold values from 0.25 to 4
- out_weight: bfloat16 [2048, 2048], P('head'), may hold values from -0.125 to 0.125
Outputs:
- layer_out: bfloat16 [2048, 2048], P('seq', 'head')
All inputs are finite; a program needn't handle non-finite values.
Results may differ from a plain program's by a relative error of at most 0.0049.
Values may be sent and summed in bfloat16 or wider, within the bound.
A program may use at most 128 MiB of HBM per device.

v0:
```python
import functools

import jax
import jax.numpy as jnp
from jax import lax
from jax.experimental import pallas as pl
from jax.experimental.pallas import tpu as pltpu
from jax.sharding import PartitionSpec as P

MESH = pl.DeviceIdType.MESH
EPS = 1e-06


def split(value):
    high = value.astype(jnp.bfloat16)
    return high, (value - high.astype(jnp.float32)).astype(jnp.bfloat16)


def product(left, right, dims=((1,), (0,))):
    return lax.dot_general(left, right, (dims, ((), ())), preferred_element_type=jnp.float32)


def row_sum(value):
    return jnp.sum(value, axis=-1, keepdims=True)


def kernel(
    seqs, groups, heads,
    q_any, k_any, v_any, ridge_ref, w_any, out_ref,
    q_ref, k_ref, v_ref, w_own, w_other,
    high_ref, low_ref, sums, sums_out, sums_in, run_out, run_in, past_out, past_in,
    qn_ref, first, mixed, mixed_in, part_out, part_in,
    load_sem, w_sem, ws_sem, wr_sem, ss_sem, sr_sem, rs_sem, rr_sem, as_sem, ar_sem, ms_sem, mr_sem, ps_sem, pr_sem,
):
    seq, group = lax.axis_index("seq"), lax.axis_index("head")
    rank, side = seq // 2, seq % 2
    pair, lane = group // 2, group % 2
    ranks, pairs = seqs // 2, groups // 2
    tokens, width = out_ref.shape
    hd = q_ref.shape[1] // heads
    twin_seq, twin_head = seq + 1 - 2 * side, group + 1 - 2 * lane
    not_first, not_last = rank > 0, rank < ranks - 1

    loads = [
        pltpu.make_async_copy(src, dst, load_sem.at[at])
        for at, (src, dst) in enumerate(((k_any, k_ref), (v_any, v_ref), (q_any, q_ref)))
    ]
    for load in loads:
        load.start()

    def columns(at, parity):
        return pl.ds(pl.multiple_of((2 * at + parity) * width, 128), width)

    w_loads = [
        pltpu.make_async_copy(w_any.at[:, columns(at, lane)], w_own.at[at], w_sem.at[at])
        for at in range(pairs)
    ]
    for load in w_loads:
        load.start()

    barrier = pltpu.get_barrier_semaphore()

    def greet(**device):
        pl.semaphore_signal(barrier, inc=1, device_id=device, device_id_type=MESH)

    greet(seq=twin_seq)
    greet(head=twin_head)
    for off in range(1, pairs):
        greet(head=2 * ((pair + off) % pairs) + lane)

    @pl.when(not_first)
    def _():
        greet(seq=seq - 2)

    @pl.when(not_last)
    def _():
        greet(seq=seq + 2)

    w_sends = [
        pltpu.make_async_remote_copy(
            w_any.at[:, columns(at, 1 - lane)], w_other.at[at], ws_sem.at[at], wr_sem.at[at],
            device_id={"head": twin_head}, device_id_type=MESH,
        )
        for at in range(pairs)
    ]

    loads[0].wait()
    loads[1].wait()
    near, far = side, 1 - side
    sum_sends = []
    for at in range(heads):
        span = slice(at * hd, (at + 1) * hd)
        keys = k_ref[:, span].astype(jnp.float32)
        scale = lax.rsqrt(row_sum(keys * keys) + EPS)
        payload = jnp.concatenate(
            [keys * (scale * scale), v_ref[:, span].astype(jnp.float32) * scale], axis=1
        )
        high, low = split(payload)
        high_ref[at] = high
        low_ref[at] = low
        both = ((0,), (0,))
        total = product(k_ref[:, span], high, both) + product(k_ref[:, span], low, both)
        sums[0, at] = total[:, :hd]
        sums[1, at] = total[:, hd:]
        sums_out[at] = sums[far, at].astype(jnp.bfloat16)
        if at == 0:
            pl.semaphore_wait(
                barrier, pairs + 1 + not_first.astype(jnp.int32) + not_last.astype(jnp.int32)
            )
        send = pltpu.make_async_remote_copy(
            sums_out.at[at], sums_in.at[at], ss_sem.at[at], sr_sem.at[at],
            device_id={"seq": twin_seq}, device_id_type=MESH,
        )
        send.start()
        sum_sends.append(send)

    for send in w_sends:
        send.start()

    causal = lax.broadcasted_iota(jnp.int32, (tokens, tokens), 0) >= lax.broadcasted_iota(
        jnp.int32, (tokens, tokens), 1
    )

    def within(at, parts):
        keys = k_ref[:, at * hd:(at + 1) * hd]
        across = ((1,), (1,))
        scores = product(parts[0], keys, across) + product(parts[1], keys, across)
        high, low = split(jnp.where(causal, scores, 0.0))
        payload = high_ref[at]
        return product(high, payload) + product(low, payload) + product(high, low_ref[at])

    loads[2].wait()
    for at in range(heads):
        q = q_ref[:, at * hd:(at + 1) * hd].astype(jnp.float32)
        q = q * lax.rsqrt(row_sum(q * q) + EPS)
        qn_ref[at] = q
        first[at] = within(at, split(q))

    bits = run_out.shape[1]
    bit = hd // bits
    run_sends = [
        [
            pltpu.make_async_remote_copy(
                run_out.at[at, piece], run_in.at[at, piece],
                rs_sem.at[at, piece], rr_sem.at[at, piece],
                device_id={"seq": (seq + 2) % seqs}, device_id_type=MESH,
            )
            for piece in range(bits)
        ]
        for at in range(heads)
    ]
    past_sends = [
        [
            pltpu.make_async_remote_copy(
                past_out.at[at, piece], past_in.at[at, piece],
                as_sem.at[at, piece], ar_sem.at[at, piece],
                device_id={"seq": twin_seq}, device_id_type=MESH,
            )
            for piece in range(bits)
        ]
        for at in range(heads)
    ]

    @pl.when(rank == 0)
    def _():
        run_in[...] = jnp.zeros(run_in.shape, run_in.dtype)

    def advance(at):
        sum_sends[at].wait_recv()
        for piece in range(bits):
            span = slice(piece * bit, (piece + 1) * bit)

            @pl.when(not_first)
            def _():
                run_sends[at][piece].wait_recv()

            @pl.when(not_last)
            def _():
                run_out[at, piece] = run_in[at, piece] + (
                    sums[near, at, span] + sums_in[at, span].astype(jnp.float32)
                )
                run_sends[at][piece].start()

            mine = jnp.where(side == 0, sums[near, at, span], 0.0)
            past_out[at, piece] = (run_in[at, piece] + mine).astype(jnp.bfloat16)
            past_sends[at][piece].start()

    mixed_sends = []

    def solve(at):
        before = jnp.where(side == 1, sums_in[at].astype(jnp.float32), 0.0)
        held, rest = split(run_in[at].reshape(hd, hd) + before)
        for piece in range(bits):
            past_sends[at][piece].wait_recv()
        given = past_in[at].reshape(hd, hd)
        none = jnp.zeros((hd, hd), jnp.bfloat16)
        left = side == 0
        state = jnp.concatenate(
            [
                jnp.concatenate([jnp.where(left, held, given), jnp.where(left, given, held)], axis=1),
                jnp.concatenate([jnp.where(left, rest, none), jnp.where(left, none, rest)], axis=1),
            ],
            axis=0,
        )

        def carried(parts):
            high, low = parts
            return product(jnp.concatenate([high, high], axis=1), state) + product(
                jnp.concatenate([low, low], axis=1), state
            )

        ridge = ridge_ref[at]
        q = qn_ref[at]
        whole = first[at] + carried(split(q))
        norm = row_sum(q * q)
        applied = whole[:, :hd] + ridge * q
        step = norm / (row_sum(q * applied) + EPS)
        residual = q - step * applied
        fresh = row_sum(residual * residual)
        direction = residual + fresh / (norm + EPS) * q
        parts = split(direction)
        again = within(at, parts) + carried(parts)
        applied = again[:, :hd] + ridge * direction
        after = fresh / (row_sum(direction * applied) + EPS)
        span = slice(at * hd, (at + 1) * hd)
        mixed[:, span] = (step * whole[:, hd:] + after * again[:, hd:]).astype(jnp.bfloat16)
        send = pltpu.make_async_remote_copy(
            mixed.at[:, span], mixed_in.at[:, span], ms_sem.at[at], mr_sem.at[at],
            device_id={"head": twin_head}, device_id_type=MESH,
        )
        send.start()
        mixed_sends.append(send)

    advance(0)
    for at in range(1, heads):
        advance(at)
        solve(at - 1)
    solve(heads - 1)

    for load in w_loads:
        load.wait()
    for send in w_sends:
        send.wait_recv()
    for send in mixed_sends[:-1]:
        send.wait_recv()
    most = (heads - 1) * hd

    def begun(index, rows):
        return product(mixed[rows, :], w_own[index]) + product(
            mixed_in[rows, :most], w_other[index, :most, :]
        )

    def ended(index, rows):
        return product(mixed_in[rows, most:], w_other[index, most:, :])

    cuts = part_out.shape[1]
    cut = tokens // cuts
    part_sends = []
    pieces = [slice(piece * cut, (piece + 1) * cut) for piece in range(cuts)]
    order = [(pair + off) % pairs for off in range(1, pairs)]
    starts = [[begun(target, rows) for rows in pieces] for target in order]
    mixed_sends[-1].wait_recv()
    for off, target in enumerate(order):
        for piece, rows in enumerate(pieces):
            part_out[off, piece] = (starts[off][piece] + ended(target, rows)).astype(jnp.bfloat16)
            send = pltpu.make_async_remote_copy(
                part_out.at[off, piece], part_in.at[off, piece],
                ps_sem.at[off, piece], pr_sem.at[off, piece],
                device_id={"head": 2 * target + lane}, device_id_type=MESH,
            )
            send.start()
            part_sends.append(send)
    own = [begun(pair, rows) + ended(pair, rows) for rows in pieces]
    for piece, rows in enumerate(pieces):
        total = own[piece]
        for off in range(pairs - 1):
            part_sends[off * cuts + piece].wait_recv()
            total = total + part_in[off, piece].astype(jnp.float32)
        out_ref[rows, :] = total.astype(out_ref.dtype)

    for send in sum_sends + w_sends + mixed_sends + part_sends + sum(past_sends, []):
        send.wait_send()

    @pl.when(not_last)
    def _():
        for send in sum(run_sends, []):
            send.wait_send()


def solution(mesh):
    seqs, groups = mesh.shape["seq"], mesh.shape["head"]

    def shards(queries, keys, values, ridges, out_weight):
        tokens, wide = queries.shape
        heads = ridges.shape[0]
        hd = wide // heads
        rows, model = out_weight.shape
        width = model // groups
        pairs = groups // 2
        cuts, bits = 4, 2
        bf16, f32 = jnp.bfloat16, jnp.float32
        dma = pltpu.SemaphoreType.DMA
        others = max(pairs - 1, 1)
        any_spec = pl.BlockSpec(memory_space=pl.ANY)
        return pl.pallas_call(
            functools.partial(kernel, seqs, groups, heads),
            out_shape=jax.ShapeDtypeStruct((tokens, width), bf16),
            in_specs=[any_spec, any_spec, any_spec, pl.BlockSpec(memory_space=pltpu.SMEM), any_spec],
            out_specs=pl.BlockSpec(memory_space=pltpu.VMEM),
            scratch_shapes=[
                pltpu.VMEM((tokens, wide), bf16),
                pltpu.VMEM((tokens, wide), bf16),
                pltpu.VMEM((tokens, wide), bf16),
                pltpu.VMEM((pairs, rows, width), bf16),
                pltpu.VMEM((pairs, rows, width), bf16),
                pltpu.VMEM((heads, tokens, 2 * hd), bf16),
                pltpu.VMEM((heads, tokens, 2 * hd), bf16),
                pltpu.VMEM((2, heads, hd, hd), f32),
                pltpu.VMEM((heads, hd, hd), bf16),
                pltpu.VMEM((heads, hd, hd), bf16),
                pltpu.VMEM((heads, bits, hd // bits, hd), f32),
                pltpu.VMEM((heads, bits, hd // bits, hd), f32),
                pltpu.VMEM((heads, bits, hd // bits, hd), bf16),
                pltpu.VMEM((heads, bits, hd // bits, hd), bf16),
                pltpu.VMEM((heads, tokens, hd), f32),
                pltpu.VMEM((heads, tokens, 2 * hd), f32),
                pltpu.VMEM((tokens, wide), bf16),
                pltpu.VMEM((tokens, wide), bf16),
                pltpu.VMEM((others, cuts, tokens // cuts, width), bf16),
                pltpu.VMEM((others, cuts, tokens // cuts, width), bf16),
                dma((3,)), dma((pairs,)), dma((pairs,)), dma((pairs,)),
                dma((heads,)), dma((heads,)),
                dma((heads, bits)), dma((heads, bits)), dma((heads, bits)), dma((heads, bits)),
                dma((heads,)), dma((heads,)), dma((others, cuts)), dma((others, cuts)),
            ],
            compiler_params=pltpu.CompilerParams(
                collective_id=0, has_side_effects=True, vmem_limit_bytes=63 * 2**20
            ),
        )(queries, keys, values, ridges, out_weight)

    in_specs = (P("seq", "head"), P("seq", "head"), P("seq", "head"), P("head"), P("head", None))
    return jax.shard_map(
        shards, mesh=mesh, in_specs=in_specs, out_specs=P("seq", "head"), check_vma=False
    )
```

profile of v0, /device:TPU:25, one launch (start us, length us, event | category | flops | bytes accessed | tf_op | source)
XLA Modules:
  0.0 35.5 jit_solution(10813711424903633867)
XLA Ops:
  0.0 33.9 %shard_map.55 = bf16[256,512]{1,0:T(8,128)(2,1)} custom-call(bf16[256,512]{1,0:T(8,128)(2,1)} %q_any.1, bf16[256,512]{1,0:T(8,128)(2,1)} %k_any.1, bf16[256,512]{1,0:T(8,128)(2,1)} %v_any.1, f32[4]{0:T(128)} %ridge_ref.1, bf16[512,2048]{1,0:T(8,128)(2,1)} %w_any.1), custom_call_target="tpu_custom_call" | custom-call | tf_op jit(solution)/shard_map/pallas_call | solution.py:305
  33.9 1.7 %copy.7 = bf16[256,512]{1,0:T(8,128)(2,1)} copy(bf16[256,512]{1,0:T(8,128)(2,1)} %shard_map.55) | data formatting | bytes 524288
where the time goes:
time: 35.7 us; the launch traced here: 35.5 us
  Pallas kernels  33.9 us (95%)
  local copies, waits for them, and re-layouts  1.67 us (5%)
    pallas_call x1, Pallas kernels, shards(): pl.pallas_call(functools.partial(kernel, seqs, groups, heads), out_shape=...  33.9 us
    unnamed x1, local copies, waits for them, and re-layouts  1.67 us

commit v1 on v0

v1 whole, which is shorter than its diff:
```python
import functools

import jax
import jax.numpy as jnp
from jax import lax
from jax.experimental import pallas as pl
from jax.experimental.pallas import tpu as pltpu
from jax.sharding import PartitionSpec as P

MESH = pl.DeviceIdType.MESH
EPS = 1e-06


def split(value):
    high = value.astype(jnp.bfloat16)
    return high, (value - high.astype(jnp.float32)).astype(jnp.bfloat16)


def product(left, right, dims=((1,), (0,))):
    return lax.dot_general(left, right, (dims, ((), ())), preferred_element_type=jnp.float32)


def row_sum(value):
    return jnp.sum(value, axis=-1, keepdims=True)


def kernel(
    seqs, groups, heads,
    q_any, k_any, v_any, ridge_any, w_any, out_ref,
    ridge_ref, q_ref, k_ref, v_ref, weight,
    high_ref, low_ref, sums, sums_out, sums_in, run_out, run_in, past_out, past_in,
    qn_ref, first, mixed, total_ref,
    load_sem, w_sem, ws_sem, wr_sem, cs_sem, cr_sem, fs_sem, fr_sem,
    ss_sem, sr_sem, xs_sem, xr_sem, rs_sem, rr_sem, as_sem, ar_sem,
    ms_sem, mr_sem, ps_sem, pr_sem, gs_sem, gr_sem,
):
    seq, group = lax.axis_index("seq"), lax.axis_index("head")
    rank, side = seq // 2, seq % 2
    pair, lane = group // 2, group % 2
    ranks, pairs = seqs // 2, groups // 2
    tokens, width = out_ref.shape
    hd = q_ref.shape[1] // heads
    twin_seq, twin_head = seq + 1 - 2 * side, group + 1 - 2 * lane
    not_first, not_last = rank > 0, rank < ranks - 1

    loads = [
        pltpu.make_async_copy(src, dst, load_sem.at[at])
        for at, (src, dst) in enumerate(
            ((k_any, k_ref), (v_any, v_ref), (q_any, q_ref), (ridge_any, ridge_ref))
        )
    ]
    for load in loads:
        load.start()

    def columns(at, parity):
        return pl.ds(pl.multiple_of((2 * at + parity) * width, 128), width)

    w_load = pltpu.make_async_copy(w_any.at[:, columns(pair, lane)], weight.at[0], w_sem)
    w_load.start()

    barrier = pltpu.get_barrier_semaphore()

    def greet(**device):
        pl.semaphore_signal(barrier, inc=1, device_id=device, device_id_type=MESH)

    greet(seq=twin_seq)
    greet(head=twin_head)
    for off in range(1, pairs):
        for parity in range(2):
            greet(head=2 * ((pair + off) % pairs) + parity)

    @pl.when(not_first)
    def _():
        greet(seq=seq - 2)

    @pl.when(not_last)
    def _():
        greet(seq=seq + 2)

    w_send = pltpu.make_async_remote_copy(
        w_any.at[:, columns(pair, 1 - lane)], weight.at[1], ws_sem, wr_sem,
        device_id={"head": twin_head}, device_id_type=MESH,
    )
    shares = 2 if ranks % 2 == 0 else 1
    parts = 2
    part = hd // parts
    blocks = parts * heads // shares
    turn = rank % shares
    cross_sends, relays = [], []
    for block in range(blocks):
        for flip in range(2):
            for off in range(1, pairs):
                target = (pair + off) % pairs
                parity = lane if flip == 0 else 1 - lane
                slot = 2 * (pairs - off) + flip
                row = pl.ds(pl.multiple_of((turn * blocks + block) * part, part), part)
                index = (slot - 2) * blocks + block
                cross_sends.append(
                    pltpu.make_async_remote_copy(
                        w_any.at[row, columns(target, parity)], weight.at[slot, row],
                        cs_sem.at[index], cr_sem.at[index],
                        device_id={"head": 2 * target + parity}, device_id_type=MESH,
                    )
                )
                relays.append(
                    pltpu.make_async_remote_copy(
                        weight.at[slot, row], weight.at[slot, row],
                        fs_sem.at[index], fr_sem.at[index],
                        device_id={"seq": seq + 2 - 4 * (rank % 2)}, device_id_type=MESH,
                    )
                )

    def relay(index):
        cross_sends[index].wait_recv()
        if shares == 2:
            relays[index].start()

    pl.semaphore_wait(barrier, 2 * pairs + not_first.astype(jnp.int32) + not_last.astype(jnp.int32))
    for send in cross_sends:
        send.start()
    w_send.start()

    loads[0].wait()
    loads[1].wait()
    near, far = side, 1 - side
    sum_sends, extra_sends = [], []
    for at in range(heads):
        span = slice(at * hd, (at + 1) * hd)
        keys = k_ref[:, span].astype(jnp.float32)
        scale = lax.rsqrt(row_sum(keys * keys) + EPS)
        payload = jnp.concatenate(
            [keys * (scale * scale), v_ref[:, span].astype(jnp.float32) * scale], axis=1
        )
        high, low = split(payload)
        high_ref[at] = high
        low_ref[at] = low
        both = ((0,), (0,))
        total = product(k_ref[:, span], high, both) + product(k_ref[:, span], low, both)
        sums[0, at] = total[:, :hd]
        sums[1, at] = total[:, hd:]
        sums_out[0, at] = total[:, :hd].astype(jnp.bfloat16)
        sums_out[1, at] = total[:, hd:].astype(jnp.bfloat16)
        send = pltpu.make_async_remote_copy(
            sums_out.at[far, at], sums_in.at[far, at], ss_sem.at[at], sr_sem.at[at],
            device_id={"seq": twin_seq}, device_id_type=MESH,
        )
        send.start()
        sum_sends.append(send)
        extra_sends.append(
            pltpu.make_async_remote_copy(
                sums_out.at[0, at], sums_in.at[0, at], xs_sem.at[at], xr_sem.at[at],
                device_id={"seq": twin_seq}, device_id_type=MESH,
            )
        )

    @pl.when(side == 0)
    def _():
        for send in extra_sends:
            send.start()


    causal = lax.broadcasted_iota(jnp.int32, (tokens, tokens), 0) >= lax.broadcasted_iota(
        jnp.int32, (tokens, tokens), 1
    )

    def within(at, parts):
        keys = k_ref[:, at * hd:(at + 1) * hd]
        across = ((1,), (1,))
        scores = product(parts[0], keys, across) + product(parts[1], keys, across)
        high, low = split(jnp.where(causal, scores, 0.0))
        payload = high_ref[at]
        return product(high, payload) + product(low, payload) + product(high, low_ref[at])

    bits = run_out.shape[1]
    bit = hd // bits
    run_sends = [
        [
            pltpu.make_async_remote_copy(
                run_out.at[at, piece], run_in.at[at, piece],
                rs_sem.at[at, piece], rr_sem.at[at, piece],
                device_id={"seq": (seq + 2) % seqs}, device_id_type=MESH,
            )
            for piece in range(bits)
        ]
        for at in range(heads)
    ]
    past_sends = [
        [
            pltpu.make_async_remote_copy(
                past_out.at[at, piece], past_in.at[at, piece],
                as_sem.at[at, piece], ar_sem.at[at, piece],
                device_id={"seq": twin_seq}, device_id_type=MESH,
            )
            for piece in range(bits)
        ]
        for at in range(heads)
    ]

    def gathered(at):
        sum_sends[at].wait_recv()
        sums[near, at] += sums_in[near, at].astype(jnp.float32)

    @pl.when(rank == 0)
    def _():
        past_out[...] = jnp.zeros(past_out.shape, past_out.dtype)
        past_in[...] = jnp.zeros(past_in.shape, past_in.dtype)
        for at in range(heads):
            gathered(at)

            @pl.when(not_last)
            def _():
                for piece in range(bits):
                    span = slice(piece * bit, (piece + 1) * bit)
                    run_out[at, piece] = sums[near, at, span].astype(run_out.dtype)
                    run_sends[at][piece].start()

    loads[2].wait()
    loads[3].wait()
    for at in range(heads):
        q = q_ref[:, at * hd:(at + 1) * hd].astype(jnp.float32)
        q = q * lax.rsqrt(row_sum(q * q) + EPS)
        qn_ref[at] = q
        first[at] = within(at, split(q))

    behind = len(relays) - 2
    for index in range(behind):

        @pl.when(index < rank)
        def _():
            relay(index)

    @pl.when(not_first)
    def _():
        for at in range(heads):
            gathered(at)
        for at in range(heads):
            for piece in range(bits):
                span = slice(piece * bit, (piece + 1) * bit)
                run_sends[at][piece].wait_recv()
                past_out[at, piece] = run_in[at, piece].astype(past_out.dtype)
                past_sends[at][piece].start()

                @pl.when(not_last)
                def _():
                    run_out[at, piece] = (
                        run_in[at, piece].astype(jnp.float32) + sums[near, at, span]
                    ).astype(run_out.dtype)
                    run_sends[at][piece].start()

    @pl.when(side == 1)
    def _():
        for send in extra_sends:
            send.wait_recv()

    for index in range(behind):

        @pl.when(index >= rank)
        def _():
            relay(index)

    mixed_sends, cross_mixed, relay_mixed = [], [], []

    def solve(at):
        @pl.when(not_first)
        def _():
            for piece in range(bits):
                past_sends[at][piece].wait_recv()

        given, held = past_in[at].reshape(hd, hd), past_out[at].reshape(hd, hd)
        left = side == 0
        none = jnp.zeros((hd, hd), jnp.bfloat16)
        state = jnp.concatenate(
            [
                jnp.concatenate([jnp.where(left, held, given), jnp.where(left, given, held)], axis=1),
                jnp.concatenate(
                    [jnp.where(left, none, sums_in[0, at]), jnp.where(left, none, sums_in[1, at])], axis=1
                ),
            ],
            axis=0,
        )

        def carried(parts):
            high, low = parts
            return product(jnp.concatenate([high, high], axis=1), state) + product(
                jnp.concatenate([low, low], axis=1), state
            )

        ridge = ridge_ref[at]
        q = qn_ref[at]
        whole = first[at] + carried(split(q))
        norm = row_sum(q * q)
        applied = whole[:, :hd] + ridge * q
        step = norm / (row_sum(q * applied) + EPS)
        residual = q - step * applied
        fresh = row_sum(residual * residual)
        direction = residual + fresh / (norm + EPS) * q
        parts = split(direction)
        again = within(at, parts) + carried(parts)
        applied = again[:, :hd] + ridge * direction
        after = fresh / (row_sum(direction * applied) + EPS)
        span = slice(at * hd, (at + 1) * hd)
        mixed[0, :, span] = (step * whole[:, hd:] + after * again[:, hd:]).astype(jnp.bfloat16)
        for off in range(1, pairs):
            target, slot = (pair + off) % pairs, 2 * (pairs - off)
            index = (pairs - off - 1) * heads + at
            send = pltpu.make_async_remote_copy(
                mixed.at[0, :, span], mixed.at[slot, :, span], ps_sem.at[index], pr_sem.at[index],
                device_id={"head": 2 * target + lane}, device_id_type=MESH,
            )
            send.start()
            cross_mixed.append(send)
            relay_mixed.append(
                pltpu.make_async_remote_copy(
                    mixed.at[slot, :, span], mixed.at[slot + 1, :, span],
                    gs_sem.at[index], gr_sem.at[index],
                    device_id={"head": twin_head}, device_id_type=MESH,
                )
            )
        send = pltpu.make_async_remote_copy(
            mixed.at[0, :, span], mixed.at[1, :, span], ms_sem.at[at], mr_sem.at[at],
            device_id={"head": twin_head}, device_id_type=MESH,
        )
        send.start()
        mixed_sends.append(send)

    for at in range(heads):
        solve(at)
        if at < 2:
            relay(behind + at)

    def pass_on(at):
        for index in range(at * (pairs - 1), (at + 1) * (pairs - 1)):
            cross_mixed[index].wait_recv()
            relay_mixed[index].start()

    pass_on(0)
    w_load.wait()
    total_ref[...] = product(mixed[0], weight[0])
    pass_on(1)
    w_send.wait_recv()
    for send in mixed_sends:
        send.wait_recv()
    total_ref[...] += product(mixed[1], weight[1])
    for at in range(2, heads):
        pass_on(at)
    if shares == 2:
        for send in relays:
            send.wait_recv()
    most = (heads - 1) * hd
    early, late = relay_mixed[:(heads - 1) * (pairs - 1)], relay_mixed[(heads - 1) * (pairs - 1):]
    for slot in range(2, 2 * pairs, 2):
        total_ref[...] += product(mixed[slot], weight[slot])
    for send in early:
        send.wait_recv()
    for slot in range(3, 2 * pairs, 2):
        total_ref[...] += product(mixed[slot, :, :most], weight[slot, :most, :])
    for send in late:
        send.wait_recv()
    total = total_ref[...]
    for slot in range(3, 2 * pairs, 2):
        total = total + product(mixed[slot, :, most:], weight[slot, most:, :])
    out_ref[...] = total.astype(out_ref.dtype)

    for send in sum_sends + [w_send] + cross_sends + mixed_sends + cross_mixed + relay_mixed:
        send.wait_send()
    if shares == 2:
        for send in relays:
            send.wait_send()

    @pl.when(side == 0)
    def _():
        for send in extra_sends:
            send.wait_send()

    @pl.when(not_first)
    def _():
        for send in sum(past_sends, []):
            send.wait_send()

    @pl.when(not_last)
    def _():
        for send in sum(run_sends, []):
            send.wait_send()


def solution(mesh):
    seqs, groups = mesh.shape["seq"], mesh.shape["head"]

    def shards(queries, keys, values, ridges, out_weight):
        tokens, wide = queries.shape
        heads = ridges.shape[0]
        hd = wide // heads
        rows, model = out_weight.shape
        width = model // groups
        pairs = groups // 2
        bits = 2
        crossing = max(4 * (pairs - 1) * (heads // (2 if (seqs // 2) % 2 == 0 else 1)), 1)
        others = max((pairs - 1) * heads, 1)
        bf16, f32 = jnp.bfloat16, jnp.float32
        wire = bf16 if seqs <= 8 else f32
        near_by = [pltpu.with_memory_space_constraint(each, pltpu.HBM) for each in (queries, keys, values, ridges, out_weight)]
        dma = pltpu.SemaphoreType.DMA
        any_spec = pl.BlockSpec(memory_space=pl.ANY)
        return pl.pallas_call(
            functools.partial(kernel, seqs, groups, heads),
            out_shape=jax.ShapeDtypeStruct((tokens, width), bf16),
            in_specs=[any_spec] * 5,
            out_specs=pl.BlockSpec(memory_space=pltpu.VMEM),
            scratch_shapes=[
                pltpu.SMEM((heads,), f32),
                pltpu.VMEM((tokens, wide), bf16),
                pltpu.VMEM((tokens, wide), bf16),
                pltpu.VMEM((tokens, wide), bf16),
                pltpu.VMEM((groups, rows, width), bf16),
                pltpu.VMEM((heads, tokens, 2 * hd), bf16),
                pltpu.VMEM((heads, tokens, 2 * hd), bf16),
                pltpu.VMEM((2, heads, hd, hd), f32),
                pltpu.VMEM((2, heads, hd, hd), bf16),
                pltpu.VMEM((2, heads, hd, hd), bf16),
                pltpu.VMEM((heads, bits, hd // bits, hd), wire),
                pltpu.VMEM((heads, bits, hd // bits, hd), wire),
                pltpu.VMEM((heads, bits, hd // bits, hd), bf16),
                pltpu.VMEM((heads, bits, hd // bits, hd), bf16),
                pltpu.VMEM((heads, tokens, hd), f32),
                pltpu.VMEM((heads, tokens, 2 * hd), f32),
                pltpu.VMEM((groups, tokens, wide), bf16),
                pltpu.VMEM((tokens, width), f32),
                dma((4,)), dma, dma, dma,
                dma((crossing,)), dma((crossing,)), dma((crossing,)), dma((crossing,)),
                dma((heads,)), dma((heads,)), dma((heads,)), dma((heads,)),
                dma((heads, bits)), dma((heads, bits)), dma((heads, bits)), dma((heads, bits)),
                dma((heads,)), dma((heads,)), dma((others,)), dma((others,)), dma((others,)), dma((others,)),
            ],
            compiler_params=pltpu.CompilerParams(
                collective_id=0, has_side_effects=True, vmem_limit_bytes=24 * 2**20
            ),
        )(*near_by)

    in_specs = (P("seq", "head"), P("seq", "head"), P("seq", "head"), P("head"), P("head", None))
    return jax.shard_map(
        shards, mesh=mesh, in_specs=in_specs, out_specs=P("seq", "head"), check_vma=False
    )
```

time: 35.7 us -> 26.9 us (0.75)
  Pallas kernels: 33.9 us -> 26 us
  local copies, waits for them, and re-layouts: 1.67 us -> 0.71 us
    pallas_call x1, Pallas kernels: 33.9 us -> 26 us  [shards(): pl.pallas_call(functools.partial(kernel, seqs, groups, heads), out_shape=...]
    unnamed x1, local copies, waits for them, and re-layouts: 1.67 us -> 0.71 us
where the time goes in v1:
time: 26.9 us; the launch traced here: 26.8 us
  Pallas kernels  26 us (97%)
  local copies, waits for them, and re-layouts  0.71 us (3%)
    pallas_call x1, Pallas kernels, shards(): pl.pallas_call(functools.partial(kernel, seqs, groups, heads), out_shape=...  26 us
    unnamed x1, local copies, waits for them, and re-layouts  0.71 us

profile of v1, /device:TPU:25, one launch (start us, length us, event | category | flops | bytes accessed | tf_op | source)
XLA Modules:
  0.0 26.8 jit_solution(612087975294773481)
XLA Ops:
  0.0 26.0 %shard_map.55 = bf16[256,512]{1,0:T(8,128)(2,1)S(1)} custom-call(bf16[256,512]{1,0:T(8,128)(2,1)} %q_any.1, bf16[256,512]{1,0:T(8,128)(2,1)} %k_any.1, bf16[256,512]{1,0:T(8,128)(2,1)} %v_any.1, f32[4]{0:T(128)} %ridge_any.1, bf16[512,2048]{1,0:T(8,128)(2,1)} %w_any.1), custom_call_target="tpu_custom_call" | custom-call | tf_op jit(solution)/shard_map/pallas_call | solution.py:404
  26.1 0.7 %copy.7 = bf16[256,512]{1,0:T(8,128)(2,1)} copy(bf16[256,512]{1,0:T(8,128)(2,1)S(1)} %shard_map.55) | data formatting | bytes 524288
